TPU v7x, 32 devices: a whole 2x2x4 slice. The times are simulated.
32 devices in a mesh: grp: 2 (over z_hi), seq: 8 (over y, x, core), tp: 2 (over z_lo).
Axes of the slice: x: 2, y: 2, z: 4 (z_hi: 2, z_lo: 2; z = z_hi * 2 + z_lo), core: 2. Of those that a mesh axis runs over, the one named last changes fastest.
Arguments:
- latents: bfloat16 [2, 64, 2048], P('grp', None, 'seq'), may hold values from -6 to 6
- patch_weight: bfloat16 [128, 5120], replicated, may hold values from -0.5 to 0.5
- patch_bias: float32 [5120], replicated, may hold values from -3 to 3
- modulation: float32 [3, 5120], replicated, may hold values from -3 to 3
- qkv_weight: bfloat16 [5120, 3, 1024], P(None, None, 'seq'), may hold values from -0.078125 to 0.078125
- norm_gain: float32 [2, 1024], P(None, 'seq'), may hold values from 0.5 to 16
- out_weight: bfloat16 [1024, 5120], P('seq', ('grp', 'tp')), may hold values from -0.5 to 0.5
- token_order: int32 [2048], replicated, may hold values from 0 to 2047, each once
- window_start: int32 [1], replicated, may hold values from 0 to 1024
Outputs:
- attended: bfloat16 [1024, 5120], P('seq', ('grp', 'tp'))
Inputs may be any that keep to these rules, and one draw needn't show every extreme that they name: Position j of the target layout holds frame-major token token_order[j]; every token stands once. The window covers target positions window_start[0] to window_start[0] + 1023.
All inputs are finite; a program needn't handle non-finite values.
Results may differ from a plain program's by a relative error of at most 0.018.
The roundings to bfloat16 on the way count: a program that leaves them out, or rounds other values in their place, can miss the bound.
Values may be sent and summed in bfloat16 or wider, within the bound.
A program may use at most 128 MiB of HBM per device.

v0:
```python
import math
import jax
import jax.numpy as jnp
from jax import lax
from jax.sharding import PartitionSpec as P

QW_DEV = 128
norm_eps = 0.1


def swapped(block, axis, apart):
    count = lax.axis_size(axis)
    route = []
    for low in range(count):
        high = low | 1 << apart
        if high != low and high < count:
            route += [(low, high), (high, low)]
    return lax.ppermute(block, axis, route)


def joined(array, axis, combine):
    everything = jax.tree.map(lambda part: lax.all_gather(part, axis), array)
    initial = jax.tree.map(lambda part: part[0], everything)

    def step(k, so_far):
        return combine(so_far, jax.tree.map(lambda part: part[k], everything))

    return lax.fori_loop(1, lax.axis_size(axis), step, initial)


def embed_rows(columns, patch_weight, patch_bias, modulation):
    channels = columns.shape[1]
    weight = patch_weight.reshape(2, channels, patch_weight.shape[1])
    embedded = (
        lax.dot_general(
            columns, weight, (((0, 1), (0, 1)), ((), ())), preferred_element_type=jnp.float32
        )
        + patch_bias
    )
    centre = embedded - jnp.mean(embedded, axis=1, keepdims=True)
    spread = jnp.mean(centre * centre, axis=1, keepdims=True)
    normed = centre * lax.rsqrt(spread + norm_eps) * (1.0 + modulation[1]) + modulation[0]
    return normed.astype(jnp.bfloat16)


def project_rows(columns, flat_weight, patch_weight, patch_bias, modulation):
    row_total = columns.shape[2]
    block = math.gcd(row_total, 512)

    def one_block(block_index):
        section = lax.dynamic_slice_in_dim(columns, block_index * block, block, 2)
        normed = embed_rows(section, patch_weight, patch_bias, modulation)
        return jnp.dot(normed, flat_weight, preferred_element_type=jnp.float32)

    result = lax.map(one_block, jnp.arange(row_total // block))
    return result.reshape(row_total, flat_weight.shape[1])


def per_device(
    latents,
    patch_weight,
    patch_bias,
    modulation,
    qkv_weight,
    norm_gain,
    out_weight,
    token_order,
    window_start,
):
    head_dim = qkv_weight.shape[2]
    seq_count = lax.axis_size("seq")
    groups = lax.axis_size("grp") * lax.axis_size("tp")
    quarter = lax.axis_index("grp") * lax.axis_size("tp") + lax.axis_index("tp")
    partner = swapped(latents, "grp", 0)
    is_high = lax.axis_index("grp") == 0
    paired = jnp.where(
        is_high, jnp.concatenate([latents, partner], 0), jnp.concatenate([partner, latents], 0)
    )
    gathered = lax.all_gather(paired, "seq", axis=2, tiled=True)
    tokens = gathered.shape[2]
    key_count = tokens // groups
    flat_weight = qkv_weight.reshape(qkv_weight.shape[0], 3 * head_dim)
    key_columns = lax.dynamic_slice_in_dim(gathered, quarter * key_count, key_count, 2)
    pair_raw = project_rows(
        key_columns, flat_weight[:, head_dim:], patch_weight, patch_bias, modulation
    )
    key_raw = pair_raw[:, :head_dim]
    values = pair_raw[:, head_dim:].astype(jnp.bfloat16)
    window_len = QW_DEV * seq_count
    window_rows = lax.dynamic_slice_in_dim(token_order, window_start[0], window_len)
    part_len = window_len // groups
    query_rows = lax.dynamic_slice_in_dim(window_rows, quarter * part_len, part_len)
    query_columns = jnp.take(gathered, query_rows, axis=2)
    query_raw = project_rows(
        query_columns, flat_weight[:, :head_dim], patch_weight, patch_bias, modulation
    )
    query_total, key_total = lax.psum(
        (jnp.sum(query_raw * query_raw, axis=1), jnp.sum(key_raw * key_raw, axis=1)), "seq"
    )
    norm_width = head_dim * seq_count
    queries = (
        query_raw * lax.rsqrt(query_total[:, None] / norm_width + norm_eps) * norm_gain[0]
    ).astype(jnp.bfloat16)
    key_rows = (
        key_raw * lax.rsqrt(key_total[:, None] / norm_width + norm_eps) * norm_gain[1]
    ).astype(jnp.bfloat16)
    queries = lax.all_gather(queries, ("grp", "tp"), axis=0, tiled=True)
    query_len = queries.shape[0]
    query_block = math.gcd(query_len, 512)
    score_scale = head_dim ** (-0.5)

    def attend(block_index):
        query_part = lax.dynamic_slice_in_dim(queries, block_index * query_block, query_block, 0)
        scores = (
            lax.dot_general(
                query_part, key_rows, (((1,), (1,)), ((), ())), preferred_element_type=jnp.float32
            )
            * score_scale
        )
        row_max = jnp.max(scores, axis=1)
        probs = jnp.exp(scores - row_max[:, None])
        row_sum = jnp.sum(probs, axis=1)
        row_acc = jnp.dot(probs.astype(jnp.bfloat16), values, preferred_element_type=jnp.float32)
        return (row_max, row_sum, row_acc)

    maxima, sums, accums = lax.map(attend, jnp.arange(query_len // query_block))
    maxima = maxima.reshape(query_len)
    sums = sums.reshape(query_len)
    accums = accums.reshape(query_len, head_dim)

    def combine(first, second):
        row_max = jnp.maximum(first[0], second[0])
        first_factor = jnp.exp(first[0] - row_max)
        second_factor = jnp.exp(second[0] - row_max)
        row_sum = first[1] * first_factor + second[1] * second_factor
        row_acc = first[2] * first_factor[:, None] + second[2] * second_factor[:, None]
        return (row_max, row_sum, row_acc)

    row_max, row_sum, row_acc = joined((maxima, sums, accums), ("grp", "tp"), combine)
    attention = (row_acc / row_sum[:, None]).astype(jnp.bfloat16)
    cols_dev = out_weight.shape[1]
    gate_cols = lax.dynamic_slice_in_dim(modulation[2], quarter * cols_dev, cols_dev)
    regrouped = lax.all_to_all(attention, "seq", split_axis=0, concat_axis=1, tiled=True)
    mixed_out = jnp.dot(
        regrouped,
        lax.all_gather(out_weight, "seq", axis=0, tiled=True),
        preferred_element_type=jnp.float32,
    )
    return (mixed_out * gate_cols).astype(jnp.bfloat16)


def solution(mesh):
    in_specs = (
        P("grp", None, "seq"),
        P(),
        P(),
        P(),
        P(None, None, "seq"),
        P(None, "seq"),
        P("seq", ("grp", "tp")),
        P(),
        P(),
    )
    out_specs = P("seq", ("grp", "tp"))
    return jax.shard_map(
        per_device, mesh=mesh, in_specs=in_specs, out_specs=out_specs, check_vma=False
    )
```

profile of v0, /device:TPU:0, one launch (start us, length us, event | category | flops | bytes accessed | tf_op | source)
XLA Modules:
  0.0 168.9 jit_solution(8679716140680726561)
XLA Ops:
  6.5 0.0 copy-start
  6.5 0.0 all-gather.5.cloned.1.call-start
  6.5 4.1 %collective-permute-start = (bf16[1,64,256]{2,1,0:T(8,128)(2,1)}, bf16[1,64,256]{2,1,0:T(8,128)(2,1)S(1)}, u32[]{:S(2)}, u32[]{:S(2)}) collective-permute-start(bf16[1,64,256]{2,1,0:T(8,128)(2,1)} %param.13), channel_id=1, source_target_pairs={{0,16},{16,0},{1,17},{17,1},{2,18},{18,2},{3,19},{19,3},{4,20},{20... | collective-permute-start | bytes 98312 | tf_op jit(solution)/shard_map/ppermute | solution.py:18
  11.3 1.7 %fusion.22 = (f32[1,5120]{1,0:T(1,128)}, f32[1,5120]{1,0:T(1,128)S(1)}, f32[1,5120]{1,0:T(1,128)S(1)}) fusion(f32[3,5120]{1,0:T(4,128)} %param.16), kind=kLoop, calls=%fused_computation.62 | loop fusion | flops 5120 | bytes 122880 | tf_op jit(solution)/shard_map/slice | solution.py:142
  13.0 1.3 slice_bitcast_fusion.1
  14.4 1.3 compare_and_fusion
  15.7 6.3 %copy.28 = bf16[5120,3,128]{0,2,1:T(8,128)(2,1)} copy(bf16[5120,3,128]{2,0,1:T(8,128)(2,1)} %param.17) | data formatting | bytes 7864320 | tf_op args[4]
  22.0 0.0 collective-permute-done
  22.0 0.0 copy-done.4
  22.0 10.9 %all_gather.18 = bf16[2,64,2048]{2,1,0:T(8,128)(2,1)S(1)} all-gather(bf16[2,64,256]{2,1,0:T(8,128)(2,1)S(1)} %maximum_select_fusion), channel_id=1, replica_groups=mesh['grp'=2,'seq'=8,'tp'=2] {'seq'}, dimensions={2}, use_global_device_ids=true | all-gather | bytes 589824 | tf_op jit(solution)/shard_map/all_gather | solution.py:79
  33.0 0.7 copy.26
  33.7 0.0 copy-done
  33.7 0.0 copy-done.3
  33.7 1.6 fusion.9
  35.4 1.6 multiply_reduce_fusion
  37.0 0.0 copy-done.5
  37.0 0.0 copy-done.7
  37.0 0.5 copy-done.1
  37.5 2.5 %fusion.11 = f32[512,256]{0,1:T(8,128)S(1)} fusion(f32[512,5120,1]{1,0,2:T(8,128)S(1)} %get-tuple-element.357, f32[5120]{0:T(1024)S(1)} %bitcast.97, f32[5120]{0:T(1024)S(1)} %bitcast.95, f32[512]{0:T(512)S(1)} %add_rsqrt_fusion.1, f32[512]{0:T(512)S(1)} %broadcast_multiply_fusion, f32[5120]{0:T(1024)S(1)} %copy-done.3, bf16[5120,384]{0,1:T(8,128)(2,1)S(1)} %bitcast.83), kind=kOutput, calls=%fused_computation.26 | convolution fusion | flops 1357905920 | bytes 13697024 | tf_op jit(solution)/shard_map/while/body/eval_jaxpr/dot_general | solution.py:53
  40.1 1.6 gather_fusion
  41.7 1.2 fusion.19
  42.9 0.0 copy-start.6
  42.9 0.0 copy-start.8
  42.9 1.7 %fusion.23 = (f32[256]{0:T(256)S(1)}, f32[256,5120]{1,0:T(8,128)S(1)}) fusion(f32[5120]{0:T(1024)} %param.15, bf16[2,64,5120]{2,1,0:T(8,128)(2,1)S(1)} %bitcast.80, bf16[2,64,256]{1,0,2:T(2,128)(2,1)S(1)} %fusion.19), kind=kOutput, calls=%fused_computation.63 | convolution fusion | flops 338165504 | bytes 6640640 | tf_op jit(solution)/shard_map/while/body/eval_jaxpr/dot_general | solution.py:35
  44.6 0.7 multiply_reduce_fusion.1
  45.3 0.0 copy-start.9
  45.3 0.0 copy-done.6
  45.4 0.0 copy-done.8
  45.4 2.6 %multiply_reduce_fusion.3 = (f32[256]{0:T(256)S(1)}, f32[256,128]{0,1:T(8,128)S(1)}) fusion(bf16[5120,384]{0,1:T(8,128)(2,1)} %bitcast.82, f32[256,5120]{1,0:T(8,128)S(1)} %get-tuple-element.353, f32[5120]{0:T(1024)S(1)} %bitcast.98, f32[5120]{0:T(1024)S(1)} %bitcast.96, f32[256]{0:T(256)S(1)} %add_rsqrt_fusion.3, f32[256]{0:T(256)S(1)} %broadcast_multiply_fusion.1), kind=kOutput, calls=%fused_computation.42 | convolution fusion | flops 342163200 | bytes 6728704 | tf_op jit(solution)/shard_map/while/body/eval_jaxpr/dot_general | solution.py:53
  47.9 13.2 %all-reduce = (f32[256]{0:T(256)S(1)}, f32[512]{0:T(512)S(1)}) all-reduce(f32[256]{0:T(256)S(1)} %get-tuple-element.354, f32[512]{0:T(512)S(1)} %multiply_reduce_fusion.2), channel_id=1, replica_groups=mesh['grp'=2,'seq'=8,'tp'=2] {'seq'}, use_global_device_ids=true, to_apply=%region_3.4 | all-reduce | flops 768 | bytes 6144 | tf_op jit(solution)/shard_map/psum | solution.py:97
  61.1 0.1 multiply_convert_fusion
  61.2 0.1 copy.30
  61.4 0.1 multiply_convert_fusion.1
  61.5 14.4 %all_gather.19 = bf16[1024,128]{0,1:T(8,128)(2,1)S(1)} all-gather(bf16[256,128]{0,1:T(8,128)(2,1)S(1)} %multiply_convert_fusion.1), channel_id=1, replica_groups=mesh['grp'=2,'seq'=8,'tp'=2] {'grp','tp'}, dimensions={0}, use_global_device_ids=true | all-gather | bytes 327680 | tf_op jit(solution)/shard_map/all_gather | solution.py:107
  75.9 0.1 copy.31
  76.0 4.4 %while.11 = (s32[]{:T(128)}, f32[2,512]{1,0:T(2,128)S(1)}, f32[2,512]{1,0:T(2,128)S(1)}, f32[2,512,128]{2,1,0:T(8,128)S(1)}, s32[2]{0:T(128)S(1)}, /*index=5*/bf...) while((s32[]{:T(128)}, f32[2,512]{1,0:T(2,128)S(1)}, ...), condition=%wide.region_11.12_spmd, body=%wide.region_8.11_spmd.sunk | while | flops 135789568 | bytes 3817663 | solution.py:126
  76.0 0.6 dynamic_slice.81
  77.2 0.3 fusion.40
  77.5 0.4 fusion.42
  77.9 0.2 fusion.41
  78.2 0.6 dynamic_slice.81
  79.5 0.3 fusion.40
  79.8 0.4 fusion.42
  80.1 0.2 fusion.41
  80.4 0.0 copy-start.2
  80.4 0.8 copy-done.2
  81.2 0.0 all-gather.5.cloned.1.call-update
  81.3 0.0 all-gather.7.cloned.1.call-start
  81.3 0.7 all-gather.7.cloned.1.call-update
  82.0 13.5 %all-gather = f32[4,1,1024]{2,1,0:T(1,128)S(1)} all-gather(f32[1,1,1024]{2,1,0:T(1,128)S(1)} %reshape.73), channel_id=1, replica_groups=mesh['grp'=2,'seq'=8,'tp'=2] {'grp','tp'}, dimensions={0}, use_global_device_ids=true | all-gather | bytes 20480 | tf_op jit(solution)/shard_map/all_gather | solution.py:22
  95.6 13.8 %all-gather.1 = f32[4,1,1024]{2,1,0:T(1,128)S(1)} all-gather(f32[1,1,1024]{2,1,0:T(1,128)S(1)} %reshape.75), channel_id=1, replica_groups=mesh['grp'=2,'seq'=8,'tp'=2] {'grp','tp'}, dimensions={0}, use_global_device_ids=true | all-gather | bytes 20480 | tf_op jit(solution)/shard_map/all_gather | solution.py:22
  109.4 16.2 %all-gather.5.cloned.1.call-done = f32[4,1024,128]{2,1,0:T(8,128)} async-done(((f32[1,1024,128]{2,1,0:T(8,128)}), f32[4,1024,128]{2,1,0:T(8,128)}) %all-gather.5.cloned.1.call-update) | async-done | bytes 2097168 | tf_op jit(solution)/shard_map/all_gather | solution.py:22
  125.6 1.1 slice_bitcast_fusion
  126.7 4.7 %while.42 = (s32[]{:T(128)}, f32[1024]{0:T(1024)S(1)}, f32[1024]{0:T(1024)S(1)}, f32[1024,128]{1,0:T(8,128)S(1)}, f32[4,1024]{1,0:T(4,128)S(1)}, /*index=5*/f32[...) while((s32[]{:T(128)}, f32[1024]{0:T(1024)S(1)}, f32[1024]{0:T(1024)S(1)}, ...), condition=%wide.region_13.14_spmd, body=%wide.region_12.13_spmd.sunk | while | flops 399365 | bytes 1630359 | solution.py:28
  126.8 1.5 fusion.43
  128.3 1.5 fusion.43
  129.9 1.5 fusion.43
  131.4 0.9 divide_convert_fusion
  132.3 3.6 %all-to-all-start = ((bf16[8,128,128]{2,1,0:T(8,128)(2,1)}), bf16[8,128,128]{2,1,0:T(8,128)(2,1)S(1)}, u32[]{:S(2)}, u32[]{:S(2)}) async-start(bf16[8,128,128]{2,1,0:T(8,128)(2,1)} %bitcast.21), calls=%async_computation | async-start | bytes 524288 | tf_op jit(solution)/shard_map/all_to_all | solution.py:143
  135.9 0.7 dynamic-slice_reduce_fusion
  136.6 7.0 %all-to-all-done = bf16[8,128,128]{2,1,0:T(8,128)(2,1)S(1)} async-done(((bf16[8,128,128]{2,1,0:T(8,128)(2,1)}), bf16[8,128,128]{2,1,0:T(8,128)(2,1)S(1)}, u32[]{:S(2)}, u32[]{:S(2)}) %all-to-all-start) | async-done | bytes 262176 | tf_op jit(solution)/shard_map/all_to_all | solution.py:143
  143.6 0.2 copy.32
  143.8 15.3 %all-gather.7.cloned.1.call-done = bf16[1024,1280]{1,0:T(8,128)(2,1)} async-done(((bf16[128,1280]{1,0:T(8,128)(2,1)}), bf16[1024,1280]{1,0:T(8,128)(2,1)}) %all-gather.7.cloned.1.call-update) | async-done | bytes 2621456 | tf_op jit(solution)/shard_map/all_gather | solution.py:146
  159.1 3.0 %fusion.14 = bf16[128,1280]{1,0:T(8,128)(2,1)} fusion(bf16[128,1024]{0,1:T(8,128)(2,1)S(1)} %bitcast.84, bf16[1024,1280]{1,0:T(8,128)(2,1)} %all-gather.7.cloned.1.call-done, f32[1280]{0:T(1024)S(1)} %dynamic-slice_reduce_fusion), kind=kOutput, calls=%fused_computation.30 | convolution fusion | flops 335872000 | bytes 3216384 | tf_op jit(solution)/shard_map/dot_general | solution.py:144
  (38 shorter events, 0.4 us)
Async XLA Ops:
  6.5 27.2 %copy-start = (bf16[128,5120]{1,0:T(8,128)(2,1)S(1)}, bf16[128,5120]{1,0:T(8,128)(2,1)}, u32[]{:S(2)}) copy-start(bf16[128,5120]{1,0:T(8,128)(2,1)} %param.14) | copy-start | bytes 3932164
  6.5 15.5 %copy-start.4 = (bf16[1,64,256]{2,1,0:T(8,128)(2,1)S(1)}, bf16[1,64,256]{2,1,0:T(8,128)(2,1)}, u32[]{:S(2)}) copy-start(bf16[1,64,256]{2,1,0:T(8,128)(2,1)} %param.13) | copy-start | bytes 98308
  6.5 27.2 %copy-start.3 = (f32[5120]{0:T(1024)S(1)}, f32[5120]{0:T(1024)}, u32[]{:S(2)}) copy-start(f32[5120]{0:T(1024)} %param.15) | copy-start | bytes 61444
  6.5 119.1 %all-gather.5.cloned.1.call-start = ((), (), s32[]{:S(2)}) async-start(), calls=%async_computation.1 | async-start | bytes 2621440 | tf_op jit(solution)/shard_map/all_gather | solution.py:22
  6.5 15.5 %collective-permute-start = (bf16[1,64,256]{2,1,0:T(8,128)(2,1)}, bf16[1,64,256]{2,1,0:T(8,128)(2,1)S(1)}, u32[]{:S(2)}, u32[]{:S(2)}) collective-permute-start(bf16[1,64,256]{2,1,0:T(8,128)(2,1)} %param.13), channel_id=1, source_target_pairs={{0,16},{16,0},{1,17},{17,1},{2,18},{18,2},{3,19},{19,3},{4,20},{20... | collective-permute-start | bytes 98312 | tf_op jit(solution)/shard_map/ppermute | solution.py:18
  13.0 23.9 %copy-start.5 = (f32[1,5120]{1,0:T(1,128)}, f32[1,5120]{1,0:T(1,128)S(1)}, u32[]{:S(2)}) copy-start(f32[1,5120]{1,0:T(1,128)S(1)} %get-tuple-element.348) | copy-start | bytes 61444
  13.0 24.0 %copy-start.7 = (f32[1,5120]{1,0:T(1,128)}, f32[1,5120]{1,0:T(1,128)S(1)}, u32[]{:S(2)}) copy-start(f32[1,5120]{1,0:T(1,128)S(1)} %get-tuple-element.349) | copy-start | bytes 61444
  35.4 2.1 %copy-start.1 = (bf16[5120,3,128]{0,2,1:T(8,128)(2,1)S(1)}, bf16[5120,3,128]{0,2,1:T(8,128)(2,1)}, u32[]{:S(2)}) copy-start(bf16[5120,3,128]{0,2,1:T(8,128)(2,1)} %copy.28) | copy-start | bytes 11796484
  42.9 2.4 %copy-start.6 = (f32[1,5120]{1,0:T(1,128)S(1)}, f32[1,5120]{1,0:T(1,128)}, u32[]{:S(2)}) copy-start(f32[1,5120]{1,0:T(1,128)} %copy-done.5) | copy-start | bytes 61444
  42.9 2.4 %copy-start.8 = (f32[1,5120]{1,0:T(1,128)S(1)}, f32[1,5120]{1,0:T(1,128)}, u32[]{:S(2)}) copy-start(f32[1,5120]{1,0:T(1,128)} %copy-done.7) | copy-start | bytes 61444
  45.3 15.8 %copy-start.10 = (f32[128]{0:T(128)S(1)}, f32[128]{0:T(128)}, u32[]{:S(2)}) copy-start(f32[128]{0:T(128)} %get-tuple-element.350) | copy-start | bytes 1540
  45.3 16.0 %copy-start.9 = (f32[128]{0:T(128)S(1)}, f32[128]{0:T(128)}, u32[]{:S(2)}) copy-start(f32[128]{0:T(128)} %get-tuple-element.351) | copy-start | bytes 1540
  80.4 0.8 copy-start.2
  81.3 77.8 %all-gather.7.cloned.1.call-start = ((), (), s32[]{:S(2)}) async-start(), calls=%async_computation.2 | async-start | bytes 2949120 | tf_op jit(solution)/shard_map/all_gather | solution.py:146
  132.3 11.3 %all-to-all-start = ((bf16[8,128,128]{2,1,0:T(8,128)(2,1)}), bf16[8,128,128]{2,1,0:T(8,128)(2,1)S(1)}, u32[]{:S(2)}, u32[]{:S(2)}) async-start(bf16[8,128,128]{2,1,0:T(8,128)(2,1)} %bitcast.21), calls=%async_computation | async-start | bytes 524288 | tf_op jit(solution)/shard_map/all_to_all | solution.py:143
Sparse Core Ops, SparseCore 0:
  81.4 44.2 all-gather.4
  127.5 31.5 all-gather.6
where the time goes:
time: 170 us; the launch traced here: 169 us
  blocking collectives  65.9 us (39%)
  waiting for transfers between devices  39.2 us (23%)
  local copies, waits for them, and re-layouts  15 us (9%)
  between operations  14.3 us (8%)
  matrix products  12.8 us (8%)
  other arithmetic  12.6 us (7%)
  starting transfers between devices  7.78 us (5%)
    all_gather x2, blocking collectives, joined(): everything = jax.tree.map(lambda part: lax.all_gather(part, axis), array)  27.3 us
    all_gather x1, waiting for transfers between devices, joined(): everything = jax.tree.map(lambda part: lax.all_gather(part, axis), array)  16.2 us
    all_gather x1, waiting for transfers between devices, per_device(): lax.all_gather(out_weight, 'seq', axis=0, tiled=True)  15.3 us
    all_gather x1, blocking collectives, per_device(): queries = lax.all_gather(queries, ('grp', 'tp'), axis=0, tiled=True)  14.4 us
    psum x1, blocking collectives, per_device(): lax.psum((jnp.sum(query_raw * query_raw, axis=1), jnp.sum(key_raw * key_r...  13.2 us
    all_gather x1, blocking collectives, per_device(): gathered = lax.all_gather(paired, 'seq', axis=2, tiled=True)  10.9 us
    unnamed x27, local copies, waits for them, and re-layouts  7.73 us
    all_to_all x1, waiting for transfers between devices, per_device(): lax.all_to_all(attention, 'seq', split_axis=0, concat_axis=1, tiled=True)  6.96 us
  transfers between devices with their start and end apart: 4, of which 3 were waited for; matrix products, arithmetic and copies ran while one was open for 11% of the time, Pallas kernels for 0%

commit v1 on v0

--- a/solution.py
+++ b/solution.py
@@ -76,7 +76,9 @@
     paired = jnp.where(
         is_high, jnp.concatenate([latents, partner], 0), jnp.concatenate([partner, latents], 0)
     )
-    gathered = lax.all_gather(paired, "seq", axis=2, tiled=True)
+    gathered = jnp.concatenate(
+        lax.all_to_all(jnp.stack([paired] * lax.axis_size("seq")), "seq", 0, 0), axis=2
+    )
     tokens = gathered.shape[2]
     key_count = tokens // groups
     flat_weight = qkv_weight.reshape(qkv_weight.shape[0], 3 * head_dim)

time: 170 us -> 168 us (0.988)
  blocking collectives: 65.9 us -> 56 us
  starting transfers between devices: 7.78 us -> 11.7 us
  waiting for transfers between devices: 39.2 us -> 42.4 us
    all_gather x1 -> x0, blocking collectives: 10.9 us -> none  [per_device(): gathered = lax.all_gather(paired, 'seq', axis=2, tiled=True)]
    all_to_all x0 -> x1, starting transfers between devices: none -> 3.93 us  [per_device(): lax.all_to_all(jnp.stack([paired] * lax.axis_size('seq')), 'seq', 0, 0)]
    ppermute x1, waiting for transfers between devices: 0.01 us -> 2.45 us  [swapped(): return lax.ppermute(block, axis, route)]
  transfers between devices with their start and end apart: 4 -> 5, of which waited for: 3 -> 4; matrix products, arithmetic and copies ran while one was open for 11% -> 10% of each run, Pallas kernels for 0% -> 0%
where the time goes in v1:
time: 168 us; the launch traced here: 167 us
  blocking collectives  56 us (33%)
  waiting for transfers between devices  42.4 us (25%)
  local copies, waits for them, and re-layouts  15.1 us (9%)
  between operations  14.3 us (9%)
  other arithmetic  13.5 us (8%)
  matrix products  12.8 us (8%)
  starting transfers between devices  11.7 us (7%)
    all_gather x2, blocking collectives, joined(): everything = jax.tree.map(lambda part: lax.all_gather(part, axis), array)  27.3 us
    all_gather x1, waiting for transfers between devices, joined(): everything = jax.tree.map(lambda part: lax.all_gather(part, axis), array)  17 us
    all_gather x1, waiting for transfers between devices, per_device(): lax.all_gather(out_weight, 'seq', axis=0, tiled=True)  15.3 us
    psum x1, blocking collectives, per_device(): lax.psum((jnp.sum(query_raw * query_raw, axis=1), jnp.sum(key_raw * key_r...  14.4 us
    all_gather x1, blocking collectives, per_device(): queries = lax.all_gather(queries, ('grp', 'tp'), axis=0, tiled=True)  14.3 us
    unnamed x27, local copies, waits for them, and re-layouts  7.69 us
    all_to_all x1, waiting for transfers between devices, per_device(): lax.all_to_all(attention, 'seq', split_axis=0, concat_axis=1, tiled=True)  6.94 us
    dot_general x2, matrix products, one_block(): return jnp.dot(normed, flat_weight, preferred_element_type=jnp.float32)  5.05 us
  transfers between devices with their start and end apart: 5, of which 4 were waited for; matrix products, arithmetic and copies ran while one was open for 10% of the time, Pallas kernels for 0%

profile of v1, /device:TPU:0, one launch (start us, length us, event | category | flops | bytes accessed | tf_op | source)
XLA Modules:
  0.0 167.2 jit_solution(10222009172009704403)
XLA Ops:
  6.5 0.0 copy-start
  6.5 4.1 %collective-permute-start = (bf16[1,64,256]{2,1,0:T(8,128)(2,1)}, bf16[1,64,256]{2,1,0:T(8,128)(2,1)S(1)}, u32[]{:S(2)}, u32[]{:S(2)}) collective-permute-start(bf16[1,64,256]{2,1,0:T(8,128)(2,1)} %param.13), channel_id=1, source_target_pairs={{0,16},{16,0},{1,17},{17,1},{2,18},{18,2},{3,19},{19,3},{4,20},{20... | collective-permute-start | bytes 98312 | tf_op jit(solution)/shard_map/ppermute | solution.py:18
  10.6 2.5 %collective-permute-done = bf16[1,64,256]{2,1,0:T(8,128)(2,1)S(1)} collective-permute-done((bf16[1,64,256]{2,1,0:T(8,128)(2,1)}, bf16[1,64,256]{2,1,0:T(8,128)(2,1)S(1)}, u32[]{:S(2)}, u32[]{:S(2)}) %collective-permute-start) | collective-permute-done | bytes 32800 | tf_op jit(solution)/shard_map/ppermute | solution.py:18
  13.1 0.8 maximum_select_fusion
  13.9 0.8 stack.2
  14.7 3.9 %all-to-all-start = ((bf16[8,2,64,256]{3,2,1,0:T(8,128)(2,1)}), bf16[8,2,64,256]{3,2,1,0:T(8,128)(2,1)S(1)}, u32[]{:S(2)}, u32[]{:S(2)}) async-start(bf16[8,2,64,256]{3,2,1,0:T(8,128)(2,1)} %stack.2), calls=%async_computation | async-start | bytes 1048576 | tf_op jit(solution)/shard_map/all_to_all | solution.py:80
  18.7 0.0 all-gather.5.cloned.1.call-start
  18.7 1.7 %fusion.22 = (f32[1,5120]{1,0:T(1,128)}, f32[1,5120]{1,0:T(1,128)S(1)}, f32[1,5120]{1,0:T(1,128)S(1)}) fusion(f32[3,5120]{1,0:T(4,128)} %param.16), kind=kLoop, calls=%fused_computation.62 | loop fusion | flops 5120 | bytes 122880 | tf_op jit(solution)/shard_map/slice | solution.py:144
  21.1 0.0 copy-start.3
  21.1 6.3 %copy.29 = bf16[5120,3,128]{0,2,1:T(8,128)(2,1)} copy(bf16[5120,3,128]{2,0,1:T(8,128)(2,1)} %param.17) | data formatting | bytes 7864320 | tf_op args[4]
  27.4 1.4 compare_and_fusion
  28.8 0.0 copy-done.10
  28.8 0.6 slice_bitcast_fusion.1
  29.4 0.0 all-to-all-done
  29.4 0.8 copy.27
  30.2 1.6 fusion.9
  31.9 1.6 multiply_reduce_fusion
  33.5 0.5 copy-done.1
  34.0 2.5 %fusion.11 = f32[512,256]{0,1:T(8,128)S(1)} fusion(f32[512,5120,1]{1,0,2:T(8,128)S(1)} %get-tuple-element.357, f32[5120]{0:T(1024)S(1)} %bitcast.103, f32[5120]{0:T(1024)S(1)} %bitcast.101, f32[512]{0:T(512)S(1)} %add_rsqrt_fusion.1, f32[512]{0:T(512)S(1)} %broadcast_multiply_fusion, f32[5120]{0:T(1024)S(1)} %copy-done.3, bf16[5120,384]{0,1:T(8,128)(2,1)S(1)} %bitcast.86), kind=kOutput, calls=%fused_computation.26 | convolution fusion | flops 1357905920 | bytes 13697024 | tf_op jit(solution)/shard_map/while/body/eval_jaxpr/dot_general | solution.py:53
  36.5 1.6 gather_fusion
  38.1 1.2 fusion.19
  39.4 0.0 copy-start.5
  39.4 0.0 copy-start.7
  39.4 1.7 %fusion.23 = (f32[256]{0:T(256)S(1)}, f32[256,5120]{1,0:T(8,128)S(1)}) fusion(f32[5120]{0:T(1024)} %param.15, bf16[2,64,5120]{2,1,0:T(8,128)(2,1)S(1)} %bitcast.83, bf16[2,64,256]{1,0,2:T(2,128)(2,1)S(1)} %fusion.19), kind=kOutput, calls=%fused_computation.63 | convolution fusion | flops 338165504 | bytes 6640640 | tf_op jit(solution)/shard_map/while/body/eval_jaxpr/dot_general | solution.py:35
  41.1 0.7 multiply_reduce_fusion.1
  41.8 0.0 copy-done.5
  41.8 0.0 copy-done.7
  41.8 2.6 %multiply_reduce_fusion.3 = (f32[256]{0:T(256)S(1)}, f32[256,128]{0,1:T(8,128)S(1)}) fusion(bf16[5120,384]{0,1:T(8,128)(2,1)} %bitcast.85, f32[256,5120]{1,0:T(8,128)S(1)} %get-tuple-element.353, f32[5120]{0:T(1024)S(1)} %bitcast.104, f32[5120]{0:T(1024)S(1)} %bitcast.102, f32[256]{0:T(256)S(1)} %add_rsqrt_fusion.3, f32[256]{0:T(256)S(1)} %broadcast_multiply_fusion.1), kind=kOutput, calls=%fused_computation.42 | convolution fusion | flops 342163200 | bytes 6728704 | tf_op jit(solution)/shard_map/while/body/eval_jaxpr/dot_general | solution.py:53
  44.4 14.4 %all-reduce = (f32[256]{0:T(256)S(1)}, f32[512]{0:T(512)S(1)}) all-reduce(f32[256]{0:T(256)S(1)} %get-tuple-element.354, f32[512]{0:T(512)S(1)} %multiply_reduce_fusion.2), channel_id=1, replica_groups=mesh['grp'=2,'seq'=8,'tp'=2] {'seq'}, use_global_device_ids=true, to_apply=%region_3.4 | all-reduce | flops 768 | bytes 6144 | tf_op jit(solution)/shard_map/psum | solution.py:99
  58.8 0.1 multiply_convert_fusion
  58.9 0.1 copy.31
  59.0 0.0 copy-done.8
  59.0 0.1 multiply_convert_fusion.1
  59.1 14.3 %all_gather.15 = bf16[1024,128]{0,1:T(8,128)(2,1)S(1)} all-gather(bf16[256,128]{0,1:T(8,128)(2,1)S(1)} %multiply_convert_fusion.1), channel_id=1, replica_groups=mesh['grp'=2,'seq'=8,'tp'=2] {'grp','tp'}, dimensions={0}, use_global_device_ids=true | all-gather | bytes 327680 | tf_op jit(solution)/shard_map/all_gather | solution.py:109
  73.4 0.1 copy.32
  73.6 4.4 %while.11 = (s32[]{:T(128)}, f32[2,512]{1,0:T(2,128)S(1)}, f32[2,512]{1,0:T(2,128)S(1)}, f32[2,512,128]{2,1,0:T(8,128)S(1)}, s32[2]{0:T(128)S(1)}, /*index=5*/bf...) while((s32[]{:T(128)}, f32[2,512]{1,0:T(2,128)S(1)}, ...), condition=%wide.region_11.12_spmd, body=%wide.region_8.11_spmd.sunk | while | flops 135789568 | bytes 3817663 | solution.py:128
  73.6 0.6 dynamic_slice.81
  74.8 0.3 fusion.40
  75.1 0.4 fusion.42
  75.5 0.2 fusion.41
  75.8 0.6 dynamic_slice.81
  77.0 0.3 fusion.40
  77.3 0.4 fusion.42
  77.7 0.2 fusion.41
  78.0 0.0 copy-start.2
  78.0 0.8 copy-done.2
  78.8 0.0 all-gather.5.cloned.1.call-update
  78.8 0.0 all-gather.7.cloned.1.call-start
  78.9 0.7 all-gather.7.cloned.1.call-update
  79.6 13.5 %all-gather = f32[4,1,1024]{2,1,0:T(1,128)S(1)} all-gather(f32[1,1,1024]{2,1,0:T(1,128)S(1)} %reshape.94), channel_id=1, replica_groups=mesh['grp'=2,'seq'=8,'tp'=2] {'grp','tp'}, dimensions={0}, use_global_device_ids=true | all-gather | bytes 20480 | tf_op jit(solution)/shard_map/all_gather | solution.py:22
  93.1 13.9 %all-gather.1 = f32[4,1,1024]{2,1,0:T(1,128)S(1)} all-gather(f32[1,1,1024]{2,1,0:T(1,128)S(1)} %reshape.96), channel_id=1, replica_groups=mesh['grp'=2,'seq'=8,'tp'=2] {'grp','tp'}, dimensions={0}, use_global_device_ids=true | all-gather | bytes 20480 | tf_op jit(solution)/shard_map/all_gather | solution.py:22
  107.0 17.0 %all-gather.5.cloned.1.call-done = f32[4,1024,128]{2,1,0:T(8,128)} async-done(((f32[1,1024,128]{2,1,0:T(8,128)}), f32[4,1024,128]{2,1,0:T(8,128)}) %all-gather.5.cloned.1.call-update) | async-done | bytes 2097168 | tf_op jit(solution)/shard_map/all_gather | solution.py:22
  124.0 1.1 slice_bitcast_fusion
  125.1 4.7 %while.42 = (s32[]{:T(128)}, f32[1024]{0:T(1024)S(1)}, f32[1024]{0:T(1024)S(1)}, f32[1024,128]{1,0:T(8,128)S(1)}, f32[4,1024]{1,0:T(4,128)S(1)}, /*index=5*/f32[...) while((s32[]{:T(128)}, f32[1024]{0:T(1024)S(1)}, f32[1024]{0:T(1024)S(1)}, ...), condition=%wide.region_13.14_spmd, body=%wide.region_12.13_spmd.sunk | while | flops 399365 | bytes 1630359 | solution.py:28
  125.1 1.5 fusion.43
  126.7 1.5 fusion.43
  128.2 1.5 fusion.43
  129.7 0.9 divide_convert_fusion
  130.7 3.6 %all-to-all-start.1 = ((bf16[8,128,128]{2,1,0:T(8,128)(2,1)}), bf16[8,128,128]{2,1,0:T(8,128)(2,1)S(1)}, u32[]{:S(2)}, u32[]{:S(2)}) async-start(bf16[8,128,128]{2,1,0:T(8,128)(2,1)} %bitcast.22), calls=%async_computation.1 | async-start | bytes 524288 | tf_op jit(solution)/shard_map/all_to_all | solution.py:145
  134.3 0.7 dynamic-slice_reduce_fusion
  135.0 6.9 %all-to-all-done.1 = bf16[8,128,128]{2,1,0:T(8,128)(2,1)S(1)} async-done(((bf16[8,128,128]{2,1,0:T(8,128)(2,1)}), bf16[8,128,128]{2,1,0:T(8,128)(2,1)S(1)}, u32[]{:S(2)}, u32[]{:S(2)}) %all-to-all-start.1) | async-done | bytes 262176 | tf_op jit(solution)/shard_map/all_to_all | solution.py:145
  141.9 0.2 copy.33
  142.1 15.3 %all-gather.7.cloned.1.call-done = bf16[1024,1280]{1,0:T(8,128)(2,1)} async-done(((bf16[128,1280]{1,0:T(8,128)(2,1)}), bf16[1024,1280]{1,0:T(8,128)(2,1)}) %all-gather.7.cloned.1.call-update) | async-done | bytes 2621456 | tf_op jit(solution)/shard_map/all_gather | solution.py:148
  157.4 3.0 %fusion.14 = bf16[128,1280]{1,0:T(8,128)(2,1)} fusion(bf16[128,1024]{0,1:T(8,128)(2,1)S(1)} %bitcast.90, bf16[1024,1280]{1,0:T(8,128)(2,1)} %all-gather.7.cloned.1.call-done, f32[1280]{0:T(1024)S(1)} %dynamic-slice_reduce_fusion), kind=kOutput, calls=%fused_computation.30 | convolution fusion | flops 335872000 | bytes 3216384 | tf_op jit(solution)/shard_map/dot_general | solution.py:146
  (41 shorter events, 0.4 us)
Async XLA Ops:
  6.5 23.6 %copy-start = (bf16[128,5120]{1,0:T(8,128)(2,1)S(1)}, bf16[128,5120]{1,0:T(8,128)(2,1)}, u32[]{:S(2)}) copy-start(bf16[128,5120]{1,0:T(8,128)(2,1)} %param.14) | copy-start | bytes 3932164
  6.5 22.3 %copy-start.10 = (f32[2,128]{1,0:T(2,128)S(1)}, f32[2,128]{1,0:T(2,128)}, u32[]{:S(2)}) copy-start(f32[2,128]{1,0:T(2,128)} %param.18) | copy-start | bytes 3076
  6.5 6.5 %collective-permute-start = (bf16[1,64,256]{2,1,0:T(8,128)(2,1)}, bf16[1,64,256]{2,1,0:T(8,128)(2,1)S(1)}, u32[]{:S(2)}, u32[]{:S(2)}) collective-permute-start(bf16[1,64,256]{2,1,0:T(8,128)(2,1)} %param.13), channel_id=1, source_target_pairs={{0,16},{16,0},{1,17},{17,1},{2,18},{18,2},{3,19},{19,3},{4,20},{20... | collective-permute-start | bytes 98312 | tf_op jit(solution)/shard_map/ppermute | solution.py:18
  14.7 14.6 %all-to-all-start = ((bf16[8,2,64,256]{3,2,1,0:T(8,128)(2,1)}), bf16[8,2,64,256]{3,2,1,0:T(8,128)(2,1)S(1)}, u32[]{:S(2)}, u32[]{:S(2)}) async-start(bf16[8,2,64,256]{3,2,1,0:T(8,128)(2,1)} %stack.2), calls=%async_computation | async-start | bytes 1048576 | tf_op jit(solution)/shard_map/all_to_all | solution.py:80
  18.7 105.3 %all-gather.5.cloned.1.call-start = ((), (), s32[]{:S(2)}) async-start(), calls=%async_computation.2 | async-start | bytes 2621440 | tf_op jit(solution)/shard_map/all_gather | solution.py:22
  20.4 13.0 %copy-start.4 = (f32[1,5120]{1,0:T(1,128)}, f32[1,5120]{1,0:T(1,128)S(1)}, u32[]{:S(2)}) copy-start(f32[1,5120]{1,0:T(1,128)S(1)} %get-tuple-element.348) | copy-start | bytes 61444
  20.4 13.0 %copy-start.6 = (f32[1,5120]{1,0:T(1,128)}, f32[1,5120]{1,0:T(1,128)S(1)}, u32[]{:S(2)}) copy-start(f32[1,5120]{1,0:T(1,128)S(1)} %get-tuple-element.349) | copy-start | bytes 61444
  21.1 9.1 %copy-start.3 = (f32[5120]{0:T(1024)S(1)}, f32[5120]{0:T(1024)}, u32[]{:S(2)}) copy-start(f32[5120]{0:T(1024)} %param.15) | copy-start | bytes 61444
  31.9 2.1 %copy-start.1 = (bf16[5120,3,128]{0,2,1:T(8,128)(2,1)S(1)}, bf16[5120,3,128]{0,2,1:T(8,128)(2,1)}, u32[]{:S(2)}) copy-start(bf16[5120,3,128]{0,2,1:T(8,128)(2,1)} %copy.29) | copy-start | bytes 11796484
  39.4 2.4 %copy-start.5 = (f32[1,5120]{1,0:T(1,128)S(1)}, f32[1,5120]{1,0:T(1,128)}, u32[]{:S(2)}) copy-start(f32[1,5120]{1,0:T(1,128)} %copy-done.4) | copy-start | bytes 61444
  39.4 2.4 %copy-start.7 = (f32[1,5120]{1,0:T(1,128)S(1)}, f32[1,5120]{1,0:T(1,128)}, u32[]{:S(2)}) copy-start(f32[1,5120]{1,0:T(1,128)} %copy-done.6) | copy-start | bytes 61444
  41.8 17.0 %copy-start.9 = (f32[128]{0:T(128)S(1)}, f32[128]{0:T(128)}, u32[]{:S(2)}) copy-start(f32[128]{0:T(128)} %get-tuple-element.350) | copy-start | bytes 1540
  41.8 17.2 %copy-start.8 = (f32[128]{0:T(128)S(1)}, f32[128]{0:T(128)}, u32[]{:S(2)}) copy-start(f32[128]{0:T(128)} %get-tuple-element.351) | copy-start | bytes 1540
  78.0 0.8 copy-start.2
  78.8 78.6 %all-gather.7.cloned.1.call-start = ((), (), s32[]{:S(2)}) async-start(), calls=%async_computation.3 | async-start | bytes 2949120 | tf_op jit(solution)/shard_map/all_gather | solution.py:148
  130.7 11.3 %all-to-all-start.1 = ((bf16[8,128,128]{2,1,0:T(8,128)(2,1)}), bf16[8,128,128]{2,1,0:T(8,128)(2,1)S(1)}, u32[]{:S(2)}, u32[]{:S(2)}) async-start(bf16[8,128,128]{2,1,0:T(8,128)(2,1)} %bitcast.22), calls=%async_computation.1 | async-start | bytes 524288 | tf_op jit(solution)/shard_map/all_to_all | solution.py:145
Sparse Core Ops, SparseCore 0:
  78.9 44.9 all-gather.4
  125.9 31.4 all-gather.6
